TPU v7x, 128 devices: a whole 4x4x4 slice. The times are simulated.
128 devices in a mesh: req: 16 (over y, x), tensor: 8 (over z, core).
Axes of the slice: x: 4, y: 4, z: 4, core: 2. Of those that a mesh axis runs over, the one named last changes fastest.
Arguments:
- attn_out: bfloat16 [6144, 2048], P('req', 'tensor'), may hold values from -6 to 6
- w_out: bfloat16 [2048, 2048], P('tensor'), may hold values from -0.125 to 0.125
- residual: bfloat16 [6144, 2048], P('req'), may hold values from -6 to 6
- norm_gain: float32 [2048], replicated, may hold values from 0.5 to 1.5
- expert_ids: int32 [6144, 6], P('req'), may hold values from 0 to 63, all different within a row; in each aligned block of 384 rows (0 to 383, 384 to 767, ...) at most 54 rows name the same one
- gate_weights: bfloat16 [6144, 6], P('req'), may hold values from 0.049804688 to 0.59765625
- w_gate: bfloat16 [128, 2048, 704], P(('req', 'tensor')), may hold values from -0.125 to 0.125
- w_up: bfloat16 [128, 2048, 704], P(('req', 'tensor')), may hold values from -0.125 to 0.125
- w_down: bfloat16 [128, 704, 2048], P(('req', 'tensor')), may hold values from -0.15625 to 0.15625
- s_gate: bfloat16 [2048, 2816], P(None, 'tensor'), may hold values from -0.125 to 0.125
- s_up: bfloat16 [2048, 2816], P(None, 'tensor'), may hold values from -0.125 to 0.125
- s_down: bfloat16 [2816, 2048], P('tensor'), may hold values from -0.109375 to 0.109375
- final_gain: float32 [2048], P('tensor'), may hold values from 0.5 to 1.5
- last_pos: int32 [128], P('req'), may hold values from 0 to 6143, as said below
Outputs:
- hidden_out: bfloat16 [6144, 2048], P('req', 'tensor')
- last_rms: float32 [128], P('req')
- last_peak: float32 [128], P('req')
Inputs may be any that keep to these rules, and one draw needn't show every extreme that they name: `expert_ids`: within each device's 384 rows no expert is named by more than 54 of them, a bound that some block reaches; the 6 experts of a row differ. `last_pos`: entry q lies in the rows of index q // 8 of req; entries increase, each such group's last entry is the last of its rows, and the first entry is 0.
All inputs are finite; a program needn't handle non-finite values.
Results may differ from a plain program's by a relative error of at most 0.0065.
Values may be sent and summed in bfloat16 or wider, within the bound.
A program may use at most 192 MiB of HBM per device.

v0:
```python
import functools
import math

import jax
import jax.numpy as jnp
from jax import lax
from jax.experimental import pallas as pl
from jax.experimental.pallas import tpu as pltpu
from jax.sharding import PartitionSpec as P

EPSILON = 1e-06
MESH = pl.DeviceIdType.MESH
BF16 = jnp.bfloat16
F32 = jnp.float32
LANES = 128


def dot(a, b):
    return jnp.dot(a, b, preferred_element_type=F32)


def dot_t(a, b):
    return lax.dot_general(a, b, (((1,), (1,)), ((), ())), preferred_element_type=F32)


def silu(v):
    return v / (1.0 + jnp.exp(-v))


def column_tiles(width, tile):
    return [(start, min(tile, width - start)) for start in range(0, width, tile)]


def layer_kernel(
    dims,
    attn_hbm, wout_hbm, res_hbm, gain_hbm, ids_hbm, gw_hbm, wg_hbm, wu_hbm, wd_hbm,
    sg_hbm, su_hbm, sd_hbm, fgain_hbm, last_hbm,
    out_ref, rms_ref, peak_ref,
    attn_v, wout_v, res_v, ids_v, gw_v, wg_v, wu_v, wd_v, sg_v, su_v, sd_v, gain_ref, fgain_ref, last_ref, load_sem, wout_sem,
    pair_send, pair_recv, part_own, pair_ssem, pair_rsem,
    rs_send, rs_recv, rs_ssem, rs_rsem,
    hid_v, ag_ssem, ag_rsem, sq_col, sq_all, sq_ssem, sq_rsem, inv_v,
    normed_v, nb_ssem, nb_rsem,
    slot_t, pick_v, comb_v,
    disp_v, x_v, dp_ssem, dp_rsem, keep_sem, fw_ssem, fw_rsem,
    act_v, yp_send, yp_recv, y_own, yp_ssem, yp_rsem,
    ret_send, ret_recv, rt_ssem, rt_rsem, local_sem,
    sact_v, sp_send, sp_recv, s_own, sp_ssem, sp_rsem,
    fin_send, fin_recv, fn_ssem, fn_rsem,
    st_all, st_ssem, st_rsem,
):
    NY, NX, NZ, CP = dims["ny"], dims["nx"], dims["nz"], dims["cp"]
    NR, NT = NY * NX, 2 * NZ
    R, D = attn_v.shape[0], wout_v.shape[1]
    FB, DH = D // NT, D // 2
    F, FS, TOP = wg_v.shape[0], sg_v.shape[0], ids_v.shape[0]
    GR = NY * CP
    TN = min(256, DH)
    QD = rms_ref.shape[0]
    ORDER = [0] + sorted(range(1, NZ), key=lambda k: (min(k, NZ - k), k))
    SETS = [(0, 1), (1, NZ)] if NZ < 4 else [(0, 1), (1, 3), (3, NZ)]

    t = lax.axis_index("tensor")
    r = lax.axis_index("req")
    z, c = lax.div(t, 2), lax.rem(t, 2)
    y, x = lax.div(r, NX), lax.rem(r, NX)
    sib = {"tensor": 2 * z + 1 - c}

    def zmod(k):
        return lax.rem(z + k, NZ)

    def zdev(k):
        return {"tensor": 2 * zmod(k) + c}

    def plane(dy, dx):
        return {"req": lax.rem(y + dy, NY) * NX + lax.rem(x + dx, NX)}

    def offset(i):
        dy = lax.rem(i, NY)
        return dy, lax.rem(lax.div(i, NY) + dy, NX)

    def ahead(i):
        return plane(*offset(i))

    def behind(i):
        dy, dx = offset(i)
        return plane(NY - dy, NX - dx)

    def remote(src, dst, ssem, rsem, device):
        return pltpu.make_async_remote_copy(
            src_ref=src, dst_ref=dst, send_sem=ssem, recv_sem=rsem,
            device_id=device, device_id_type=MESH,
        )

    def mul(v, n):
        return pl.multiple_of(v, n)

    def block_cols(kz, core):
        return pl.ds(mul(zmod(kz) * 2 * FB + core * FB, FB), FB)

    def half_cols(j, core, count=1):
        return pl.ds(mul(core * DH + j * FB, FB), count * FB)

    own_half = pl.ds(mul(c * DH, DH), DH)

    barrier = pltpu.get_barrier_semaphore()
    for j in range(1, NT):
        pl.semaphore_signal(barrier, inc=1, device_id={"tensor": lax.rem(t + j, NT)}, device_id_type=MESH)

    @pl.loop(1, NR)
    def _(i):
        pl.semaphore_signal(barrier, inc=1, device_id=ahead(i), device_id_type=MESH)

    loads = [
        pltpu.make_async_copy(src, dst, load_sem.at[n])
        for n, (src, dst) in enumerate([
            (attn_hbm, attn_v), (sd_hbm, sd_v), (ids_hbm, ids_v), (gw_hbm, gw_v),
            (res_hbm.at[:, pl.ds(mul(t * FB, FB), FB)], res_v),
            (gain_hbm, gain_ref), (wd_hbm.at[0], wd_v), (fgain_hbm, fgain_ref), (last_hbm, last_ref),
        ])
    ]
    blocked = [(sg_hbm, sg_v), (su_hbm, su_v), (wg_hbm.at[0], wg_v), (wu_hbm.at[0], wu_v)]
    RS_ORDER = ORDER[::-1]
    weights_in = {}
    loads[0].start()
    for core in (1, 0):
        for kz in RS_ORDER:
            cols = block_cols(kz, c if core == 0 else 1 - c)
            weights_in[core, kz] = pltpu.make_async_copy(
                wout_hbm.at[:, cols], wout_v.at[:, cols], wout_sem.at[core, kz]
            )
            weights_in[core, kz].start()
    for load in loads[2:5]:
        load.start()

    loads[0].wait()
    pair = {}
    for kz in RS_ORDER:
        weights_in[1, kz].wait()
        pair_send[kz] = dot(attn_v[...], wout_v[:, block_cols(kz, 1 - c)]).astype(BF16)
        if not pair:
            pl.semaphore_wait(barrier, NT - 1 + NR - 1)
        pair[kz] = remote(pair_send.at[kz], pair_recv.at[kz], pair_ssem.at[kz], pair_rsem.at[kz], sib)
        pair[kz].start()

    for load in loads[5:] + loads[1:2]:
        load.start()
    for n, (src, dst) in enumerate(blocked):
        for core in range(2):
            for j in range(NZ):
                pltpu.make_async_copy(
                    src.at[:, block_cols(ORDER[j], core)], dst.at[:, half_cols(j, core)], load_sem.at[10 + n]
                ).start()

    def wait_blocked(n):
        src, dst = blocked[n]
        pltpu.make_async_copy(src, dst, load_sem.at[10 + n]).wait()

    for kz in RS_ORDER:
        weights_in[0, kz].wait()
        part_own[kz] = dot(attn_v[...], wout_v[:, block_cols(kz, c)])

    rs = []
    for kz in RS_ORDER[:-1]:
        pair[kz].wait_recv()
        rs_send[kz] = (part_own[kz] + pair_recv[kz].astype(F32)).astype(BF16)
        copy = remote(rs_send.at[kz], rs_recv.at[kz], rs_ssem.at[kz], rs_rsem.at[kz], zdev(kz))
        copy.start()
        rs.append(copy)

    loads[2].wait()
    loads[3].wait()
    place_of = lax.broadcasted_iota(jnp.int32, (NR, R), 0)
    place_dy = place_of & (NY - 1)
    place_dx = ((place_of >> int(math.log2(NY))) + place_dy) & (NX - 1)
    expert_of = ((((y + place_dy) & (NY - 1)) * NX) + ((x + place_dx) & (NX - 1))) * NZ + z
    named = jnp.zeros((NR, R), F32)
    weight = jnp.zeros((NR, R), F32)
    for k in range(TOP):
        hit = ids_v[k:k + 1, :] == expert_of
        named = named + jnp.where(hit, 1.0, 0.0)
        weight = weight + jnp.where(hit, gw_v[k:k + 1, :].astype(F32), 0.0)
    row_of = lax.broadcasted_iota(jnp.int32, (R, R), 0)
    col_of = lax.broadcasted_iota(jnp.int32, (R, R), 1)
    upper = jnp.where(row_of < col_of, 1.0, 0.0).astype(BF16)
    slot = dot(named.astype(BF16), upper)
    slot = jnp.where(named > 0.5, slot, -1.0)
    slot_t[...] = jnp.zeros_like(slot_t)
    slot_t[0:NR, :] = slot
    slot_t[NR:2 * NR, :] = weight
    table = slot_t[...].T.astype(BF16)

    @pl.loop(0, NR // NY)
    def _(g):
        place = lax.broadcasted_iota(jnp.int32, (CP, R), 0).astype(F32)
        parts = []
        for d in range(NY):
            mine = slot_t[pl.ds(g * NY + d, 1), :]
            parts.append(jnp.where(place == mine, 1.0, 0.0))
        pick_v[pl.ds(mul(g * GR, GR), GR), :] = jnp.concatenate(parts, axis=0).astype(BF16)

    for start, width in column_tiles(NR * CP, LANES):
        spot = lax.broadcasted_iota(jnp.int32, (LANES, width), 1) + start
        source = lax.broadcasted_iota(jnp.int32, (LANES, width), 0)
        first = source * CP
        inside = (spot >= first) & (spot < first + CP)
        place = jnp.sum(jnp.where(inside, spot - first, 0).astype(F32), axis=0, keepdims=True)
        slots = dot(table, jnp.where(inside, 1.0, 0.0).astype(BF16))
        first = (source - NR) * CP
        inside = (spot >= first) & (spot < first + CP)
        weights = dot(table, jnp.where(inside, 1.0, 0.0).astype(BF16))
        comb_v[:, start:start + width] = jnp.where(slots == place, weights, 0.0).astype(BF16)

    loads[4].wait()
    pair[0].wait_recv()
    for copy in rs:
        copy.wait_recv()
    step = 64

    @pl.loop(0, R // step)
    def _(m):
        rows = pl.ds(mul(m * step, step), step)
        total = part_own[0, rows, :] + pair_recv[0, rows, :].astype(F32)
        for kz in range(1, NZ):
            total = total + rs_recv[kz, rows, :].astype(F32)
        hid = (res_v[rows, :].astype(F32) + total).astype(BF16)
        hid_v[0, rows, :] = hid
        values = hid.astype(F32)
        sq_col[rows, :] = jnp.broadcast_to(jnp.sum(values * values, axis=-1, keepdims=True), (step, LANES))

    sq_all[0] = sq_col[...].T[0:8, :]
    sq = []
    for j in range(1, NT):
        copy = remote(sq_all.at[0], sq_all.at[j], sq_ssem.at[j], sq_rsem.at[j], {"tensor": lax.rem(t + j, NT)})
        copy.start()
        sq.append(copy)
    ag = [None] * NZ
    for kz in ORDER[1:]:
        j = ORDER.index(NZ - kz)
        ag[j] = remote(hid_v.at[0], hid_v.at[j], ag_ssem.at[j], ag_rsem.at[j], zdev(kz))
        if min(kz, NZ - kz) == 1:
            ag[j].start()
    squares = sq_all[0]
    for j in range(1, NT):
        sq[j - 1].wait_recv()
        squares = squares + sq_all[j]
    inverse = lax.rsqrt(squares / D + EPSILON)
    inv_v[...] = jnp.broadcast_to(inverse[0:1, :], (LANES, R)).T

    nb = []

    def norm_block(j):
        if j:
            ag[j].wait_recv()

        @pl.loop(0, R // step)
        def _(m):
            rows = pl.ds(mul(m * step, step), step)
            scale = jnp.concatenate([inv_v[rows, :]] * (FB // LANES), axis=1)
            normed_v[rows, half_cols(j, c)] = (
                hid_v[j, rows, :].astype(F32) * scale * gain_ref[:, block_cols(ORDER[j], c)]
            ).astype(BF16)

        block = normed_v.at[:, half_cols(j, c)]
        copy = remote(block, block, nb_ssem.at[j], nb_rsem.at[j], sib)
        copy.start()
        nb.append(copy)

    def dispatch_copy(i, s):
        rows = pl.ds(i * CP if isinstance(i, int) else mul(i * CP, 8), CP)
        first, stop = SETS[s]
        return remote(
            disp_v.at[rows, first * FB:stop * FB], x_v.at[rows, half_cols(first, c, stop - first)],
            dp_ssem.at[i, s], dp_rsem.at[i, s], ahead(i),
        )

    first_rows = pl.ds(0, CP)

    def keep_x(s):
        first, stop = SETS[s]
        return pltpu.make_async_copy(
            disp_v.at[first_rows, first * FB:stop * FB], x_v.at[first_rows, half_cols(first, c, stop - first)],
            keep_sem.at[s],
        )

    def dispatch(g, s):
        rows = slice(g * GR, g * GR + GR)
        for j in range(*SETS[s]):
            disp_v[rows, j * FB:(j + 1) * FB] = dot(pick_v[rows, :], normed_v[:, half_cols(j, c)]).astype(BF16)
        for i in range(g * NY, g * NY + NY):
            (dispatch_copy(i, s) if i else keep_x(s)).start()

    loads[5].wait()
    norm_block(0)
    for g in range(NX):
        dispatch(g, 0)
    near = [j for j in range(1, NZ) if min(ORDER[j], NZ - ORDER[j]) == 1]
    far = [j for j in range(1, NZ) if j not in near]
    for j in near:
        ag[j].wait_send()
    for j in far:
        ag[j].start()
    for g in range(NX):
        for s in range(1, len(SETS)):
            if g == 0:
                for j in range(*SETS[s]):
                    norm_block(j)
            dispatch(g, s)

    loads[6].wait()
    wait_blocked(2)
    wait_blocked(3)

    def forward_copy(g, s):
        first, stop = SETS[s]
        block = x_v.at[pl.ds(g * GR if isinstance(g, int) else mul(g * GR, GR), GR), half_cols(first, c, stop - first)]
        return remote(block, block, fw_ssem.at[g, s], fw_rsem.at[g, s], sib)

    def partial_copy(g, kz):
        rows = pl.ds(g * GR if isinstance(g, int) else mul(g * GR, GR), GR)
        return remote(
            yp_send.at[kz, rows, :], yp_recv.at[kz, rows, :], yp_ssem.at[g, kz], yp_rsem.at[g, kz], sib
        )

    def return_copy(i, kz):
        rows = pl.ds(i * CP if isinstance(i, int) else mul(i * CP, 8), CP)
        return remote(
            ret_send.at[kz, rows, :], ret_recv.at[kz, rows, :], rt_ssem.at[i, kz], rt_rsem.at[i, kz], behind(i)
        )

    def keep_y(kz):
        return pltpu.make_async_copy(
            ret_send.at[kz, first_rows, :], ret_recv.at[kz, first_rows, :], local_sem.at[kz]
        )

    z_far = ORDER[:0:-1]
    z_order = z_far + [0]

    def give_back(g, kz):
        rows = slice(g * GR, g * GR + GR)
        partial_copy(g, kz).wait_recv()
        ret_send[kz, rows, :] = (y_own[kz, rows, :] + yp_recv[kz, rows, :].astype(F32)).astype(BF16)
        for i in range(g * NY, g * NY + NY):
            (return_copy(i, kz) if i else keep_y(kz)).start()

    early = NX // 2

    def forward(g, s):
        for i in range(g * NY, g * NY + NY):
            if i:
                dispatch_copy(i, s).wait_recv()
            else:
                keep_x(s).wait()
        forward_copy(g, s).start()

    sets = range(len(SETS))
    for g in range(NX):
        forward(g, 0)
    for s in sets[1:]:
        forward(0, s)
    for g in range(NX):
        rows = slice(g * GR, g * GR + GR)
        for s in sets:
            forward_copy(g, s).wait_recv()
        for start, width in column_tiles(F, TN):
            gate = dot_t(x_v[rows, :], wg_v[start:start + width, :])
            up = dot_t(x_v[rows, :], wu_v[start:start + width, :])
            act_v[:, start:start + width] = (silu(gate) * up).astype(BF16)
        if g + 1 < NX:
            for s in sets[1:]:
                forward(g + 1, s)
        for kz in z_order:
            yp_send[kz, rows, :] = dot(act_v[...], wd_v[:, block_cols(kz, 1 - c)]).astype(BF16)
            partial_copy(g, kz).start()
        for kz in z_order:
            y_own[kz, rows, :] = dot(act_v[...], wd_v[:, block_cols(kz, c)])
        if 0 < g <= early:
            for kz in z_far:
                give_back(g - 1, kz)

    for kz in z_far:
        for g in range(early, NX):
            give_back(g, kz)
    for g in range(NX):
        give_back(g, 0)

    loads[1].wait()
    wait_blocked(0)
    wait_blocked(1)
    for copy in nb:
        copy.wait_recv()

    for start, width in column_tiles(FS, TN):
        gate = dot_t(normed_v[...], sg_v[start:start + width, :])
        up = dot_t(normed_v[...], su_v[start:start + width, :])
        sact_v[:, start:start + width] = (silu(gate) * up).astype(BF16)
    for kz in range(NZ):
        sp_send[kz] = dot(sact_v[...], sd_v[:, block_cols(kz, 1 - c)]).astype(BF16)
    for kz in range(NZ):
        s_own[kz] = dot(sact_v[...], sd_v[:, block_cols(kz, c)])

    shared = remote(sp_send, sp_recv, sp_ssem, sp_rsem, sib)
    shared.start()

    loads[7].wait()
    loads[8].wait()
    q_of = lax.broadcasted_iota(jnp.int32, (QD, R), 0)
    r_of = lax.broadcasted_iota(jnp.int32, (QD, R), 1) + r * R
    chosen = jnp.zeros((QD, R), F32)
    for q in range(QD):
        chosen = jnp.where((q_of == q) & (r_of == last_ref[q]), 1.0, chosen)

    shared.wait_recv()
    fin = []
    for kz in z_order:
        keep_y(kz).wait()

        @pl.loop(1, NR)
        def _(i):
            return_copy(i, kz).wait_recv()

        total = dot(comb_v[...], ret_recv[kz]) + s_own[kz] + sp_recv[kz].astype(F32)
        if not kz:
            s_own[kz] = total
        else:
            fin_send[kz] = total.astype(BF16)
            copy = remote(fin_send.at[kz], fin_recv.at[kz], fn_ssem.at[kz], fn_rsem.at[kz], zdev(kz))
            copy.start()
            fin.append(copy)

    for copy in fin:
        copy.wait_recv()

    total = s_own[0]
    for k in range(1, NZ):
        total = total + fin_recv[k].astype(F32)
    out_ref[...] = (hid_v[0].astype(F32) + total).astype(BF16)

    last = dot(chosen.astype(BF16), out_ref[...])
    squares = jnp.sum(last * last, axis=1, keepdims=True)
    peak = jnp.max(last * fgain_ref[...], axis=1, keepdims=True)
    is_first = lax.broadcasted_iota(jnp.int32, (QD, LANES), 1) == 0
    st_all[0] = jnp.where(is_first, squares, peak)
    st = []
    for j in range(1, NT):
        copy = remote(
            st_all.at[0], st_all.at[j], st_ssem.at[j], st_rsem.at[j], {"tensor": lax.rem(t + j, NT)}
        )
        copy.start()
        st.append(copy)
    squares, peak = st_all[0], st_all[0]
    for j in range(1, NT):
        st[j - 1].wait_recv()
        squares = squares + st_all[j]
        peak = jnp.maximum(peak, st_all[j])
    rms = jnp.sqrt(squares[:, 0:1] / D + EPSILON)
    rms_ref[...] = jnp.broadcast_to(rms, (QD, LANES))
    peak_ref[...] = jnp.broadcast_to(peak[:, 1:2] / rms, (QD, LANES))

    shared.wait_send()
    for copy in list(pair.values()) + rs + sq + [ag[j] for j in far] + nb + fin + st:
        copy.wait_send()

    @pl.loop(1, NR)
    def _(i):
        for s in range(len(SETS)):
            dispatch_copy(i, s).wait_send()
        for kz in range(NZ):
            return_copy(i, kz).wait_send()

    @pl.loop(0, NX)
    def _(g):
        for s in range(len(SETS)):
            forward_copy(g, s).wait_send()
        for kz in range(NZ):
            partial_copy(g, kz).wait_send()


def on_device(
    ny, cap,
    attn_out, w_out, residual, norm_gain, expert_ids, gate_weights, w_gate, w_up, w_down,
    s_gate, s_up, s_down, final_gain, last_pos,
):
    NT, NR = lax.axis_size("tensor"), lax.axis_size("req")
    NZ, NX = NT // 2, NR // ny
    CP = -(-cap // 8) * 8
    R, D = residual.shape
    FB = D // NT
    F, FS, TOP, QD = w_gate.shape[2], s_gate.shape[1], expert_ids.shape[1], last_pos.shape[0]
    SL = NR * CP
    dims = {"ny": ny, "nx": NX, "nz": NZ, "cp": CP}
    dma = pltpu.SemaphoreType.DMA
    vmem = pltpu.VMEM
    scratch = [
        vmem((R, FB), BF16), vmem((FB, D), BF16), vmem((R, FB), BF16), vmem((TOP, R), jnp.int32),
        vmem((TOP, R), BF16), vmem((F, D), BF16), vmem((F, D), BF16), vmem((F, D), BF16),
        vmem((FS, D), BF16), vmem((FS, D), BF16), vmem((FS, D), BF16),
        vmem((1, D), F32), vmem((1, FB), F32), pltpu.SMEM((QD,), jnp.int32), dma((14,)), dma((2, NZ)),
        vmem((NZ, R, FB), BF16), vmem((NZ, R, FB), BF16), vmem((NZ, R, FB), F32), dma((NZ,)), dma((NZ,)),
        vmem((NZ, R, FB), BF16), vmem((NZ, R, FB), BF16), dma((NZ,)), dma((NZ,)),
        vmem((NZ, R, FB), BF16), dma((NZ,)), dma((NZ,)),
        vmem((R, LANES), F32), vmem((NT, 8, R), F32), dma((NT,)), dma((NT,)), vmem((R, LANES), F32),
        vmem((R, D), BF16), dma((NZ,)), dma((NZ,)),
        vmem((LANES, R), F32), vmem((SL, R), BF16), vmem((R, SL), BF16),
        vmem((SL, D // 2), BF16), vmem((SL, D), BF16), dma((NR, 3)), dma((NR, 3)), dma((3,)), dma((NX, 3)), dma((NX, 3)),
        vmem((ny * CP, F), BF16), vmem((NZ, SL, FB), BF16), vmem((NZ, SL, FB), BF16), vmem((NZ, SL, FB), F32),
        dma((NX, NZ)), dma((NX, NZ)),
        vmem((NZ, SL, FB), BF16), vmem((NZ, SL, FB), BF16), dma((NR, NZ)), dma((NR, NZ)), dma((NZ,)),
        vmem((R, FS), BF16), vmem((NZ, R, FB), BF16), vmem((NZ, R, FB), BF16), vmem((NZ, R, FB), F32), dma, dma,
        vmem((NZ, R, FB), BF16), vmem((NZ, R, FB), BF16), dma((NZ,)), dma((NZ,)),
        vmem((NT, QD, LANES), F32), dma((NT,)), dma((NT,)),
    ]
    anywhere = pl.BlockSpec(memory_space=pltpu.HBM)
    inside = pl.BlockSpec(memory_space=pltpu.VMEM)
    hidden_out, last_rms, last_peak = pl.pallas_call(
        functools.partial(layer_kernel, dims),
        name="layer",
        out_shape=(
            pltpu.VMEM((R, FB), BF16),
            pltpu.VMEM((QD, LANES), F32),
            pltpu.VMEM((QD, LANES), F32),
        ),
        in_specs=[anywhere] * 14,
        out_specs=(inside, inside, inside),
        scratch_shapes=scratch,
        compiler_params=pltpu.CompilerParams(
            collective_id=0, has_side_effects=True, vmem_limit_bytes=62_000_000
        ),
    )(
        attn_out, w_out, residual, norm_gain.reshape(1, D), expert_ids.T, gate_weights.T,
        jnp.swapaxes(w_gate, 1, 2), jnp.swapaxes(w_up, 1, 2), w_down, s_gate.T, s_up.T, s_down, final_gain.reshape(1, FB), last_pos,
    )
    return hidden_out, last_rms[:, 0], last_peak[:, 0]


def solution(mesh, ny=4, cap=54):
    return jax.shard_map(
        functools.partial(on_device, ny, cap),
        mesh=mesh,
        in_specs=(
            P("req", "tensor"),
            P("tensor", None),
            P("req", None),
            P(),
            P("req", None),
            P("req", None),
            P(("req", "tensor"), None, None),
            P(("req", "tensor"), None, None),
            P(("req", "tensor"), None, None),
            P(None, "tensor"),
            P(None, "tensor"),
            P("tensor", None),
            P("tensor"),
            P("req"),
        ),
        out_specs=(P("req", "tensor"), P("req"), P("req")),
        check_vma=False,
    )
```

profile of v0, /device:TPU:1, one launch (start us, length us, event | category | flops | bytes accessed | tf_op | source)
XLA Modules:
  0.0 89.5 jit_solution(2542798595517029505)
XLA Ops:
  0.6 87.6 %layer.1 = (bf16[384,256]{1,0:T(8,128)(2,1)S(1)}, f32[8,128]{1,0:T(8,128)S(1)}, f32[8,128]{1,0:T(8,128)S(1)}) custom-call(bf16[384,256]{1,0:T(8,128)(2,1)} %attn_hbm.1, bf16[256,2048]{1,0:T(8,128)(2,1)} %wout_hbm.1, bf16[384,2048]{1,0:T(8,128)(2,1)} %res_hbm.1, f32[1,2048]{1,0:T(1,128)} %bitcast.13, s32[6,384]{1,0:T(8,128)} %bitcast.12, ...), custom_call_target="tpu_custom_call" | custom-call | tf_op jit(solution)/shard_map/layer/pallas_call | solution.py:515
  88.2 0.7 slice_reduce_fusion
  88.9 0.7 copy.18
where the time goes:
time: 89.7 us; the launch traced here: 89.5 us
  Pallas kernels  87.6 us (98%)
  local copies, waits for them, and re-layouts  1.34 us (1%)
    pallas_call x1, Pallas kernels, on_device(): pl.pallas_call(functools.partial(layer_kernel, dims), name='layer', out_s...  87.6 us

commit v1 on v0

--- a/solution.py
+++ b/solution.py
@@ -42,6 +42,7 @@
     hid_v, ag_ssem, ag_rsem, sq_col, sq_all, sq_ssem, sq_rsem, inv_v,
     normed_v, nb_ssem, nb_rsem,
     slot_t, pick_v, comb_v,
+    sc_send, sc_recv, sc_col, sc_ssem, sc_rsem,
     disp_v, x_v, dp_ssem, dp_rsem, keep_sem, fw_ssem, fw_rsem,
     act_v, yp_send, yp_recv, y_own, yp_ssem, yp_rsem,
     ret_send, ret_recv, rt_ssem, rt_rsem, local_sem,
@@ -168,6 +169,7 @@
         copy.start()
         rs.append(copy)
 
+    sc_send[...] = jnp.zeros_like(sc_send)
     loads[2].wait()
     loads[3].wait()
     place_of = lax.broadcasted_iota(jnp.int32, (NR, R), 0)
@@ -240,12 +242,56 @@
         ag[j] = remote(hid_v.at[0], hid_v.at[j], ag_ssem.at[j], ag_rsem.at[j], zdev(kz))
         if min(kz, NZ - kz) == 1:
             ag[j].start()
+    def dispatch_copy(i, s):
+        rows = pl.ds(i * CP if isinstance(i, int) else mul(i * CP, 8), CP)
+        first, stop = SETS[s]
+        return remote(
+            disp_v.at[rows, first * FB:stop * FB], x_v.at[rows, half_cols(first, c, stop - first)],
+            dp_ssem.at[i, s], dp_rsem.at[i, s], ahead(i),
+        )
+
+    first_rows = pl.ds(0, CP)
+
+    def keep_x(s):
+        first, stop = SETS[s]
+        return pltpu.make_async_copy(
+            disp_v.at[first_rows, first * FB:stop * FB], x_v.at[first_rows, half_cols(first, c, stop - first)],
+            keep_sem.at[s],
+        )
+
+    def dispatch(g, s):
+        rows = slice(g * GR, g * GR + GR)
+        for j in range(*SETS[s]):
+            block = normed_v[:, half_cols(j, c)] if j else hid_v[0]
+            disp_v[rows, j * FB:(j + 1) * FB] = dot(pick_v[rows, :], block).astype(BF16)
+        for i in range(g * NY, g * NY + NY):
+            (dispatch_copy(i, s) if i else keep_x(s)).start()
+
+    for g in range(NX):
+        dispatch(g, 0)
+
     squares = sq_all[0]
     for j in range(1, NT):
         sq[j - 1].wait_recv()
         squares = squares + sq_all[j]
     inverse = lax.rsqrt(squares / D + EPSILON)
     inv_v[...] = jnp.broadcast_to(inverse[0:1, :], (LANES, R)).T
+
+    def scale_copy(i):
+        return remote(sc_send.at[i], sc_recv.at[i], sc_ssem.at[i], sc_rsem.at[i], ahead(i))
+
+    keep_scale = pltpu.make_async_copy(sc_send.at[0], sc_recv.at[0], local_sem.at[NZ])
+    parts, left = [], inverse[0:1, :]
+    for _ in range(3):
+        part = left.astype(BF16)
+        parts.append(part)
+        left = left - part.astype(F32)
+    parts = jnp.concatenate(parts + [jnp.zeros((5, R), BF16)], axis=0)
+    for i in range(NR):
+        slots = dot_t(parts, pick_v[i * CP:(i + 1) * CP, :])
+        scale = slots[0:1, :] + slots[1:2, :] + slots[2:3, :]
+        sc_send[i, :, 0:CP] = jnp.broadcast_to(scale, (8, CP))
+        (scale_copy(i) if i else keep_scale).start()
 
     nb = []
 
@@ -266,34 +312,8 @@
         copy.start()
         nb.append(copy)
 
-    def dispatch_copy(i, s):
-        rows = pl.ds(i * CP if isinstance(i, int) else mul(i * CP, 8), CP)
-        first, stop = SETS[s]
-        return remote(
-            disp_v.at[rows, first * FB:stop * FB], x_v.at[rows, half_cols(first, c, stop - first)],
-            dp_ssem.at[i, s], dp_rsem.at[i, s], ahead(i),
-        )
-
-    first_rows = pl.ds(0, CP)
-
-    def keep_x(s):
-        first, stop = SETS[s]
-        return pltpu.make_async_copy(
-            disp_v.at[first_rows, first * FB:stop * FB], x_v.at[first_rows, half_cols(first, c, stop - first)],
-            keep_sem.at[s],
-        )
-
-    def dispatch(g, s):
-        rows = slice(g * GR, g * GR + GR)
-        for j in range(*SETS[s]):
-            disp_v[rows, j * FB:(j + 1) * FB] = dot(pick_v[rows, :], normed_v[:, half_cols(j, c)]).astype(BF16)
-        for i in range(g * NY, g * NY + NY):
-            (dispatch_copy(i, s) if i else keep_x(s)).start()
-
     loads[5].wait()
     norm_block(0)
-    for g in range(NX):
-        dispatch(g, 0)
     near = [j for j in range(1, NZ) if min(ORDER[j], NZ - ORDER[j]) == 1]
     far = [j for j in range(1, NZ) if j not in near]
     for j in near:
@@ -351,9 +371,19 @@
                 dispatch_copy(i, s).wait_recv()
             else:
                 keep_x(s).wait()
+        if s == 0:
+            rows = slice(g * GR, g * GR + GR)
+            scale = jnp.concatenate([sc_col[0:CP, 8 * i:8 * i + 1] for i in range(g * NY, g * NY + NY)], axis=0)
+            x_v[rows, half_cols(0, c)] = (
+                x_v[rows, half_cols(0, c)].astype(F32) * scale * gain_ref[:, block_cols(0, c)]
+            ).astype(BF16)
         forward_copy(g, s).start()
 
     sets = range(len(SETS))
+    keep_scale.wait()
+    for i in range(1, NR):
+        scale_copy(i).wait_recv()
+    sc_col[:, 0:8 * NR] = sc_recv[...].reshape(8 * NR, LANES).T
     for g in range(NX):
         forward(g, 0)
     for s in sets[1:]:
@@ -366,6 +396,9 @@
             gate = dot_t(x_v[rows, :], wg_v[start:start + width, :])
             up = dot_t(x_v[rows, :], wu_v[start:start + width, :])
             act_v[:, start:start + width] = (silu(gate) * up).astype(BF16)
+        if 0 < g <= early:
+            for kz in z_far:
+                give_back(g - 1, kz)
         if g + 1 < NX:
             for s in sets[1:]:
                 forward(g + 1, s)
@@ -374,9 +407,6 @@
             partial_copy(g, kz).start()
         for kz in z_order:
             y_own[kz, rows, :] = dot(act_v[...], wd_v[:, block_cols(kz, c)])
-        if 0 < g <= early:
-            for kz in z_far:
-                give_back(g - 1, kz)
 
     for kz in z_far:
         for g in range(early, NX):
@@ -463,6 +493,7 @@
 
     @pl.loop(1, NR)
     def _(i):
+        scale_copy(i).wait_send()
         for s in range(len(SETS)):
             dispatch_copy(i, s).wait_send()
         for kz in range(NZ):
@@ -502,10 +533,11 @@
         vmem((R, LANES), F32), vmem((NT, 8, R), F32), dma((NT,)), dma((NT,)), vmem((R, LANES), F32),
         vmem((R, D), BF16), dma((NZ,)), dma((NZ,)),
         vmem((LANES, R), F32), vmem((SL, R), BF16), vmem((R, SL), BF16),
+        vmem((NR, 8, LANES), F32), vmem((NR, 8, LANES), F32), vmem((LANES, LANES), F32), dma((NR,)), dma((NR,)),
         vmem((SL, D // 2), BF16), vmem((SL, D), BF16), dma((NR, 3)), dma((NR, 3)), dma((3,)), dma((NX, 3)), dma((NX, 3)),
         vmem((ny * CP, F), BF16), vmem((NZ, SL, FB), BF16), vmem((NZ, SL, FB), BF16), vmem((NZ, SL, FB), F32),
         dma((NX, NZ)), dma((NX, NZ)),
-        vmem((NZ, SL, FB), BF16), vmem((NZ, SL, FB), BF16), dma((NR, NZ)), dma((NR, NZ)), dma((NZ,)),
+        vmem((NZ, SL, FB), BF16), vmem((NZ, SL, FB), BF16), dma((NR, NZ)), dma((NR, NZ)), dma((NZ + 1,)),
         vmem((R, FS), BF16), vmem((NZ, R, FB), BF16), vmem((NZ, R, FB), BF16), vmem((NZ, R, FB), F32), dma, dma,
         vmem((NZ, R, FB), BF16), vmem((NZ, R, FB), BF16), dma((NZ,)), dma((NZ,)),
         vmem((NT, QD, LANES), F32), dma((NT,)), dma((NT,)),

time: 89.7 us -> 87.4 us (0.974)
  Pallas kernels: 87.6 us -> 85.3 us
    pallas_call x1, Pallas kernels: 87.6 us -> 85.3 us  [on_device(): pl.pallas_call(functools.partial(layer_kernel, dims), name='layer', out_s...]
where the time goes in v1:
time: 87.4 us; the launch traced here: 87.3 us
  Pallas kernels  85.3 us (98%)
  local copies, waits for them, and re-layouts  1.34 us (2%)
    pallas_call x1, Pallas kernels, on_device(): pl.pallas_call(functools.partial(layer_kernel, dims), name='layer', out_s...  85.3 us

profile of v1, /device:TPU:1, one launch (start us, length us, event | category | flops | bytes accessed | tf_op | source)
XLA Modules:
  0.0 87.3 jit_solution(13708921121770421320)
XLA Ops:
  0.6 85.3 %layer.1 = (bf16[384,256]{1,0:T(8,128)(2,1)S(1)}, f32[8,128]{1,0:T(8,128)S(1)}, f32[8,128]{1,0:T(8,128)S(1)}) custom-call(bf16[384,256]{1,0:T(8,128)(2,1)} %attn_hbm.1, bf16[256,2048]{1,0:T(8,128)(2,1)} %wout_hbm.1, bf16[384,2048]{1,0:T(8,128)(2,1)} %res_hbm.1, f32[1,2048]{1,0:T(1,128)} %bitcast.13, s32[6,384]{1,0:T(8,128)} %bitcast.12, ...), custom_call_target="tpu_custom_call" | custom-call | tf_op jit(solution)/shard_map/layer/pallas_call | solution.py:547
  85.9 0.7 slice_reduce_fusion
  86.6 0.7 copy.18

commit v2 on v1

--- a/solution.py
+++ b/solution.py
@@ -219,7 +219,7 @@
         copy.wait_recv()
     step = 64
 
-    @pl.loop(0, R // step)
+    @pl.loop(0, R // step, unroll=True)
     def _(m):
         rows = pl.ds(mul(m * step, step), step)
         total = part_own[0, rows, :] + pair_recv[0, rows, :].astype(F32)
@@ -299,7 +299,7 @@
         if j:
             ag[j].wait_recv()
 
-        @pl.loop(0, R // step)
+        @pl.loop(0, R // step, unroll=True)
         def _(m):
             rows = pl.ds(mul(m * step, step), step)
             scale = jnp.concatenate([inv_v[rows, :]] * (FB // LANES), axis=1)

time: 87.4 us -> 86.9 us (level)
  no operation moved by 1% of the time
where the time goes in v2:
time: 86.9 us; the launch traced here: 86.8 us
  Pallas kernels  84.8 us (98%)
  local copies, waits for them, and re-layouts  1.34 us (2%)
    pallas_call x1, Pallas kernels, on_device(): pl.pallas_call(functools.partial(layer_kernel, dims), name='layer', out_s...  84.8 us

profile of v2, /device:TPU:1, one launch (start us, length us, event | category | flops | bytes accessed | tf_op | source)
XLA Modules:
  0.0 86.8 jit_solution(18067795324139233949)
XLA Ops:
  0.6 84.8 %layer.1 = (bf16[384,256]{1,0:T(8,128)(2,1)S(1)}, f32[8,128]{1,0:T(8,128)S(1)}, f32[8,128]{1,0:T(8,128)S(1)}) custom-call(bf16[384,256]{1,0:T(8,128)(2,1)} %attn_hbm.1, bf16[256,2048]{1,0:T(8,128)(2,1)} %wout_hbm.1, bf16[384,2048]{1,0:T(8,128)(2,1)} %res_hbm.1, f32[1,2048]{1,0:T(1,128)} %bitcast.13, s32[6,384]{1,0:T(8,128)} %bitcast.12, ...), custom_call_target="tpu_custom_call" | custom-call | tf_op jit(solution)/shard_map/layer/pallas_call | solution.py:547
  85.4 0.7 slice_reduce_fusion
  86.1 0.7 copy.18
